TPU v7x, 32 devices: a whole 2x2x4 slice. The times are simulated.
32 devices in a mesh: groups: 2 (over x), seq: 8 (over z, y), head: 2 (over core).
Axes of the slice: x: 2, y: 2, z: 4, core: 2. Of those that a mesh axis runs over, the one named last changes fastest.
Arguments:
- queries: bfloat16 [512, 4096], P(('groups', 'seq'), 'head'), parts along dimension 0, may hold values from -24 to 24
- vision: bfloat16 [4096, 7680], P(('groups', 'seq')), parts along dimension 0, may hold values from -6 to 6
- key_matrix: bfloat16 [7680, 512], P('seq', 'head'), may hold values from -0.0625 to 0.0625
- value_matrix: bfloat16 [7680, 512], P('seq', 'head'), may hold values from -0.0625 to 0.0625
- out_weight: bfloat16 [4096, 8192], P('head', 'seq'), may hold values from -0.09375 to 0.09375
- residual: bfloat16 [512, 8192], P(('groups', 'head'), 'seq'), parts along dimension 0, may hold values from -4 to 4
- query_norm_gain: float32 [128], replicated, may hold values from 1 to 12
- key_norm_gain: float32 [128], replicated, may hold values from 1 to 12
- attn_gate: float32 [1], replicated, may hold values from 0.5 to 2
Outputs:
- mixed: bfloat16 [512, 8192], P(('groups', 'head'), 'seq'), parts along dimension 0
There are 2 independent parts, one for each index of `groups`. A program takes and returns all parts, laid end to end along the dimension named above; an argument that names none is the same for every part. Nothing has to cross between parts.
All inputs are finite; a program needn't handle non-finite values.
Results may differ from a plain program's by a relative error of at most 0.015.
The roundings to bfloat16 on the way count: a program that leaves them out, or rounds other values in their place, can miss the bound.
Values may be sent and summed in bfloat16 or wider, within the bound.
A program may use at most 64 MiB of HBM per device.

v0:
```python
import jax
import jax.numpy as jnp
from jax import lax
from jax.sharding import PartitionSpec as P

HEAD_SIZE = 128
epsilon = 1e-05


def apply_norm(value_heads, gain):
    return (
        value_heads
        * lax.rsqrt(jnp.mean(value_heads * value_heads, axis=-1, keepdims=True) + epsilon)
        * gain
    )


def body(
    queries,
    vision,
    key_matrix,
    value_matrix,
    out_weight,
    residual,
    query_norm_gain,
    key_norm_gain,
    attn_gate,
):
    vision_rows = vision.shape[0]
    column_count = key_matrix.shape[1]
    expanded_keys = jnp.dot(
        vision,
        lax.all_gather(key_matrix, "seq", axis=0, tiled=True),
        preferred_element_type=jnp.float32,
    )
    expanded_values = jnp.dot(
        vision,
        lax.all_gather(value_matrix, "seq", axis=0, tiled=True),
        preferred_element_type=jnp.float32,
    )
    kv_local = column_count // HEAD_SIZE
    key_heads = apply_norm(
        expanded_keys.reshape(vision_rows, kv_local, HEAD_SIZE), key_norm_gain
    ).astype(jnp.bfloat16)
    value_heads = expanded_values.reshape(vision_rows, kv_local, HEAD_SIZE).astype(jnp.bfloat16)
    text_rows = queries.shape[0]
    heads_local = queries.shape[1] // HEAD_SIZE
    heads_per_group = heads_local // kv_local
    norm_result = apply_norm(
        queries.astype(jnp.float32).reshape(text_rows, kv_local, heads_per_group, HEAD_SIZE),
        query_norm_gain,
    ).astype(jnp.bfloat16)
    scale = HEAD_SIZE ** (-0.5)
    start_max = jnp.full((text_rows, kv_local, heads_per_group), -1e30, jnp.float32)
    start_den = jnp.zeros((text_rows, kv_local, heads_per_group), jnp.float32)
    start_num = jnp.zeros((text_rows, kv_local, heads_per_group, HEAD_SIZE), jnp.float32)
    key_piece = lax.all_gather(key_heads, "seq", axis=0, tiled=True)
    value_piece = lax.all_gather(value_heads, "seq", axis=0, tiled=True)
    piece_rows = key_piece.shape[0]
    rows_per_block = 512
    key_blocks = key_piece.reshape(
        piece_rows // rows_per_block, rows_per_block, kv_local, HEAD_SIZE
    )
    value_blocks = value_piece.reshape(
        piece_rows // rows_per_block, rows_per_block, kv_local, HEAD_SIZE
    )

    def advance(state_now, both):
        maxima, denominator, numerator = state_now
        scores = (
            jnp.einsum("tgqd,rgd->tgqr", norm_result, both[0], preferred_element_type=jnp.float32)
            * scale
        )
        new_max = jnp.maximum(maxima, jnp.max(scores, axis=-1))
        rescale = jnp.exp(maxima - new_max)
        weights = jnp.exp(scores - new_max[..., None])
        denominator = denominator * rescale + jnp.sum(weights, axis=-1)
        numerator = numerator * rescale[..., None] + jnp.einsum(
            "tgqr,rgd->tgqd",
            weights.astype(jnp.bfloat16),
            both[1],
            preferred_element_type=jnp.float32,
        )
        return ((new_max, denominator, numerator), None)

    maxima, denominator, numerator = lax.scan(
        advance, (start_max, start_den, start_num), (key_blocks, value_blocks)
    )[0]
    attended = (
        (numerator / denominator[..., None])
        .astype(jnp.bfloat16)
        .reshape(text_rows, heads_local * HEAD_SIZE)
    )
    partial_out = jnp.dot(
        lax.all_gather(attended, "seq", axis=0, tiled=True),
        out_weight,
        preferred_element_type=jnp.float32,
    )
    projected = lax.psum_scatter(
        partial_out.astype(jnp.bfloat16), "head", scatter_dimension=0, tiled=True
    ).astype(jnp.float32)
    return (residual.astype(jnp.float32) + jnp.tanh(attn_gate[0]) * projected).astype(jnp.bfloat16)


def solution(mesh):
    in_specs = (
        P(("groups", "seq"), "head"),
        P(("groups", "seq"), None),
        P("seq", "head"),
        P("seq", "head"),
        P("head", "seq"),
        P(("groups", "head"), "seq"),
        P(),
        P(),
        P(),
    )
    out_specs = P(("groups", "head"), "seq")
    return jax.shard_map(body, mesh=mesh, in_specs=in_specs, out_specs=out_specs, check_vma=False)
```

profile of v0, /device:TPU:0, one launch (start us, length us, event | category | flops | bytes accessed | tf_op | source)
XLA Modules:
  0.0 306.7 jit_solution(3217196021253669261)
XLA Ops:
  6.5 0.7 all-gather.6.cloned.1.call-update
  7.3 0.7 all-gather.10.cloned.1.call-update
  8.1 73.7 %all-gather.6.cloned.1.call-done = bf16[7680,256]{1,0:T(8,128)(2,1)} async-done(((bf16[960,256]{1,0:T(8,128)(2,1)}), bf16[7680,256]{1,0:T(8,128)(2,1)}) %all-gather.6.cloned.1.call-update) | async-done | bytes 3932176 | tf_op jit(solution)/shard_map/all_gather | solution.py:33
  81.8 5.0 %multiply_reduce_fusion.1 = (f32[256,2]{0,1:T(2,128)S(1)}, f32[256,256]{0,1:T(8,128)S(1)}) fusion(bf16[256,7680]{1,0:T(8,128)(2,1)} %param.12, bf16[7680,256]{1,0:T(8,128)(2,1)} %all-gather.6.cloned.1.call-done), kind=kOutput, calls=%fused_computation.27 | convolution fusion | flops 1006763520 | bytes 8128512 | tf_op jit(solution)/shard_map/dot_general | solution.py:31
  86.7 0.1 copy.23
  86.9 0.8 multiply_convert_fusion.1
  87.8 64.3 %all-gather.10.cloned.1.call-done = bf16[7680,256]{1,0:T(8,128)(2,1)} async-done(((bf16[960,256]{1,0:T(8,128)(2,1)}), bf16[7680,256]{1,0:T(8,128)(2,1)}) %all-gather.10.cloned.1.call-update) | async-done | bytes 3932176 | tf_op jit(solution)/shard_map/all_gather | solution.py:38
  152.1 4.9 %convolution_convert_fusion.1 = bf16[256,256]{0,1:T(8,128)(2,1)S(1)} fusion(bf16[256,7680]{1,0:T(8,128)(2,1)} %param.12, bf16[7680,256]{1,0:T(8,128)(2,1)} %all-gather.10.cloned.1.call-done), kind=kOutput, calls=%fused_computation.20 | convolution fusion | flops 1006698496 | bytes 7995392 | tf_op jit(solution)/shard_map/dot_general | solution.py:36
  157.1 0.7 copy.26
  158.0 0.2 multiply_reduce_fusion
  158.4 0.1 multiply_convert_fusion
  158.5 34.7 %all-gather.8.cloned.1.call-done = bf16[2048,2,128]{2,0,1:T(8,128)(2,1)} async-done(((bf16[256,2,128]{2,0,1:T(8,128)(2,1)}), bf16[2048,2,128]{2,0,1:T(8,128)(2,1)}) %all-gather.8.cloned.1.call-update) | async-done | bytes 1048592 | tf_op jit(solution)/shard_map/all_gather | solution.py:57
  193.2 41.0 %all-gather.12.cloned.1.call-done = bf16[2048,2,128]{2,0,1:T(8,128)(2,1)} async-done(((bf16[256,2,128]{2,0,1:T(8,128)(2,1)}), bf16[2048,2,128]{2,0,1:T(8,128)(2,1)}) %all-gather.12.cloned.1.call-update) | async-done | bytes 1048592 | tf_op jit(solution)/shard_map/all_gather | solution.py:58
  234.3 12.4 %while.15 = (s32[]{:T(128)}, f32[32,2,8]{0,2,1:T(8,128)S(1)}, f32[32,2,8]{0,2,1:T(8,128)S(1)}, f32[32,2,8,128]{3,0,2,1:T(8,128)S(1)}, bf16[4,512,2,128]{3,1,0,2:...) while((s32[]{:T(128)}, f32[32,2,8]{0,2,1:T(8,128)S(1)}, ...), condition=%wide.region_5.6_spmd.clone, body=%wide.region_2.5_spmd.clone.sunk | while | flops 135989760 | bytes 4358265 | solution.py:86
  234.3 1.3 fusion.31
  235.6 0.3 fusion.32
  235.9 1.4 fusion.34
  237.4 1.3 fusion.31
  238.7 0.3 fusion.32
  239.0 1.4 fusion.34
  240.5 1.3 fusion.31
  241.8 0.3 fusion.32
  242.1 1.4 fusion.34
  243.6 1.3 fusion.31
  244.9 0.3 fusion.32
  245.3 1.4 fusion.34
  246.7 0.1 divide_convert_fusion
  246.9 0.7 copy.38
  247.7 39.1 %all-gather.14.cloned.1.call-done = bf16[256,2048]{1,0:T(8,128)(2,1)} async-done(((bf16[32,2048]{1,0:T(8,128)(2,1)}), bf16[256,2048]{1,0:T(8,128)(2,1)}) %all-gather.14.cloned.1.call-update) | async-done | bytes 1048592 | tf_op jit(solution)/shard_map/all_gather | solution.py:95
  286.7 4.6 %convolution_convert_fusion = bf16[256,1024]{1,0:T(8,128)(2,1)} fusion(bf16[256,2048]{1,0:T(8,128)(2,1)} %all-gather.14.cloned.1.call-done, bf16[2048,1024]{1,0:T(8,128)(2,1)} %param.15), kind=kOutput, calls=%fused_computation.19 | convolution fusion | flops 1074003968 | bytes 5767168 | tf_op jit(solution)/shard_map/dot_general | solution.py:94
  292.0 6.1 %reduce-scatter.2.cloned.1.call-done = bf16[128,1024]{1,0:T(8,128)(2,1)} async-done(((bf16[256,1024]{1,0:T(8,128)(2,1)}), bf16[128,1024]{1,0:T(8,128)(2,1)}) %reduce-scatter.2.cloned.1.call-update) | async-done | bytes 262160 | tf_op jit(solution)/shard_map/reduce_scatter | solution.py:99
  298.1 1.7 add_convert_fusion
  (41 shorter events, 0.7 us)
Async XLA Ops:
  6.5 75.2 %all-gather.6.cloned.1.call-start = ((), (), s32[]{:S(2)}) async-start(), calls=%async_computation.1 | async-start | bytes 4423680 | tf_op jit(solution)/shard_map/all_gather | solution.py:33
  7.3 144.9 %all-gather.10.cloned.1.call-start = ((), (), s32[]{:S(2)}) async-start(), calls=%async_computation.3 | async-start | bytes 4423680 | tf_op jit(solution)/shard_map/all_gather | solution.py:38
  8.0 78.9 %copy-start.2 = (f32[128]{0:T(128)S(1)}, f32[128]{0:T(128)}, u32[]{:S(2)}) copy-start(f32[128]{0:T(128)} %param.18) | copy-start | bytes 1540
  8.0 185.2 %all-gather.8.cloned.1.call-start = ((), (), s32[]{:S(2)}) async-start(), calls=%async_computation.2 | async-start | bytes 1179648 | tf_op jit(solution)/shard_map/all_gather | solution.py:57
  87.7 70.2 %copy-start.1 = (bf16[32,2048]{1,0:T(8,128)(2,1)S(1)}, bf16[32,2048]{1,0:T(8,128)(2,1)}, u32[]{:S(2)}) copy-start(bf16[32,2048]{1,0:T(8,128)(2,1)} %param.11) | copy-start | bytes 393220
  87.7 70.6 %copy-start.3 = (f32[128]{0:T(128)S(1)}, f32[128]{0:T(128)}, u32[]{:S(2)}) copy-start(f32[128]{0:T(128)} %param.17) | copy-start | bytes 1540
  87.7 146.5 %all-gather.12.cloned.1.call-start = ((), (), s32[]{:S(2)}) async-start(), calls=%async_computation.4 | async-start | bytes 1179648 | tf_op jit(solution)/shard_map/all_gather | solution.py:58
  157.8 128.9 %all-gather.14.cloned.1.call-start = ((), (), s32[]{:S(2)}) async-start(), calls=%async_computation.5 | async-start | bytes 1179648 | tf_op jit(solution)/shard_map/all_gather | solution.py:95
  247.6 50.5 %copy-start = (bf16[128,1024]{1,0:T(8,128)(2,1)S(1)}, bf16[128,1024]{1,0:T(8,128)(2,1)}, u32[]{:S(2)}) copy-start(bf16[128,1024]{1,0:T(8,128)(2,1)} %param.16) | copy-start | bytes 786436
  247.6 50.5 %reduce-scatter.2.cloned.1.call-start = ((), (), s32[]{:S(2)}) async-start(), calls=%async_computation.6 | async-start | bytes 786432 | tf_op jit(solution)/shard_map/reduce_scatter | solution.py:99
Sparse Core Ops, SparseCore 0:
  9.5 72.2 all-gather.5
  84.0 68.1 all-gather.9
  154.3 38.8 all-gather.7
  195.3 38.9 all-gather.11
  247.7 38.9 all-gather.13
  291.5 6.6 reduce-scatter.1
where the time goes:
time: 307 us
  waiting for transfers between devices  260 us (85%)
  matrix products  25.4 us (8%)
  between operations  14.3 us (5%)
  other arithmetic  4.32 us (1%)
    all_gather x1, waiting for transfers between devices, body(): lax.all_gather(key_matrix, 'seq', axis=0, tiled=True)  73.7 us
    all_gather x1, waiting for transfers between devices, body(): lax.all_gather(value_matrix, 'seq', axis=0, tiled=True)  64.3 us
    all_gather x1, waiting for transfers between devices, body(): value_piece = lax.all_gather(value_heads, 'seq', axis=0, tiled=True)  41 us
    all_gather x1, waiting for transfers between devices, body(): lax.all_gather(attended, 'seq', axis=0, tiled=True)  39.1 us
    all_gather x1, waiting for transfers between devices, body(): key_piece = lax.all_gather(key_heads, 'seq', axis=0, tiled=True)  34.7 us
  transfers between devices with their start and end apart: 6, of which 6 were waited for; matrix products, arithmetic and copies ran while one was open for 4% of the time, Pallas kernels for 0%

commit v1 on v0

--- a/solution.py
+++ b/solution.py
@@ -26,6 +26,23 @@
     key_norm_gain,
     attn_gate,
 ):
+
+    def supply_all_loops(base_x, out_dim=0):
+        comm_axis = "seq"
+        axis_total = jax.lax.axis_size(comm_axis)
+        shelf = []
+        for src_i in range(1, axis_total):
+            shelf.append((src_i - 1, src_i))
+        next_value = shelf + [(axis_total - 1, 0)]
+        extra = base_x
+        nodes = [extra]
+        for _ in range(axis_total - 1):
+            extra = jax.lax.ppermute(extra, axis_name=comm_axis, perm=next_value)
+            nodes += [extra]
+        reached = jnp.concatenate([*reversed(nodes)], out_dim)
+        spare = jax.lax.axis_index(comm_axis)
+        return jnp.roll(reached, (spare + 1) * extra.shape[out_dim], out_dim)
+
     vision_rows = vision.shape[0]
     column_count = key_matrix.shape[1]
     expanded_keys = jnp.dot(
@@ -55,7 +72,7 @@
     start_den = jnp.zeros((text_rows, kv_local, heads_per_group), jnp.float32)
     start_num = jnp.zeros((text_rows, kv_local, heads_per_group, HEAD_SIZE), jnp.float32)
     key_piece = lax.all_gather(key_heads, "seq", axis=0, tiled=True)
-    value_piece = lax.all_gather(value_heads, "seq", axis=0, tiled=True)
+    value_piece = supply_all_loops(value_heads)
     piece_rows = key_piece.shape[0]
     rows_per_block = 512
     key_blocks = key_piece.reshape(

time: 307 us -> 284 us (0.925)
  waiting for transfers between devices: 260 us -> 240 us
  matrix products: 25.4 us -> 21.5 us
    ppermute x0 -> x7, waiting for transfers between devices: none -> 48.9 us  [supply_all_loops(): extra = jax.lax.ppermute(extra, axis_name=comm_axis, perm=next_value)]
    all_gather x1 -> x0, waiting for transfers between devices: 41 us -> none  [body(): value_piece = lax.all_gather(value_heads, 'seq', axis=0, tiled=True)]
    all_gather x1, waiting for transfers between devices: 73.7 us -> 36.2 us  [body(): lax.all_gather(key_matrix, 'seq', axis=0, tiled=True)]
    all_gather x1, waiting for transfers between devices: 64.3 us -> 73.7 us  [body(): lax.all_gather(value_matrix, 'seq', axis=0, tiled=True)]
    dot_general x4, matrix products: 5.6 us -> 1.72 us  [advance(): jnp.einsum('tgqr,rgd->tgqd', weights.astype(jnp.bfloat16), both[1], prefe...]
  transfers between devices with their start and end apart: 6 -> 12, of which waited for: 6 -> 11; matrix products, arithmetic and copies ran while one was open for 4% -> 4% of each run, Pallas kernels for 0% -> 0%
where the time goes in v1:
time: 284 us; the launch traced here: 283 us
  waiting for transfers between devices  240 us (85%)
  matrix products  21.5 us (8%)
  between operations  14.1 us (5%)
  other arithmetic  4.29 us (2%)
    all_gather x1, waiting for transfers between devices, body(): lax.all_gather(value_matrix, 'seq', axis=0, tiled=True)  73.7 us
    ppermute x7, waiting for transfers between devices, supply_all_loops(): extra = jax.lax.ppermute(extra, axis_name=comm_axis, perm=next_value)  48.9 us
    all_gather x1, waiting for transfers between devices, body(): lax.all_gather(attended, 'seq', axis=0, tiled=True)  39.1 us
    all_gather x1, waiting for transfers between devices, body(): lax.all_gather(key_matrix, 'seq', axis=0, tiled=True)  36.2 us
    all_gather x1, waiting for transfers between devices, body(): key_piece = lax.all_gather(key_heads, 'seq', axis=0, tiled=True)  34.4 us
    reduce_scatter x1, waiting for transfers between devices, body(): lax.psum_scatter(partial_out.astype(jnp.bfloat16), 'head', scatter_dimens...  6.1 us
  transfers between devices with their start and end apart: 12, of which 11 were waited for; matrix products, arithmetic and copies ran while one was open for 4% of the time, Pallas kernels for 0%

profile of v1, /device:TPU:0, one launch (start us, length us, event | category | flops | bytes accessed | tf_op | source)
XLA Modules:
  0.0 283.5 jit_solution(5833378277156233884)
XLA Ops:
  6.5 0.7 all-gather.9.cloned.1.call-update
  7.3 0.7 all-gather.5.cloned.1.call-update
  8.1 73.7 %all-gather.9.cloned.1.call-done = bf16[7680,256]{1,0:T(8,128)(2,1)} async-done(((bf16[960,256]{1,0:T(8,128)(2,1)}), bf16[7680,256]{1,0:T(8,128)(2,1)}) %all-gather.9.cloned.1.call-update) | async-done | bytes 3932176 | tf_op jit(solution)/shard_map/all_gather | solution.py:55
  81.8 4.9 %convolution_convert_fusion.1 = bf16[256,256]{0,1:T(8,128)(2,1)S(1)} fusion(bf16[256,7680]{1,0:T(8,128)(2,1)} %param.12, bf16[7680,256]{1,0:T(8,128)(2,1)} %all-gather.9.cloned.1.call-done), kind=kOutput, calls=%fused_computation.20 | convolution fusion | flops 1006698496 | bytes 7995392 | tf_op jit(solution)/shard_map/dot_general | solution.py:53
  86.8 0.6 collective-permute-start
  87.5 7.2 %collective-permute-done = bf16[256,2,128]{2,0,1:T(8,128)(2,1)S(1)} collective-permute-done((bf16[256,2,128]{2,0,1:T(8,128)(2,1)S(1)}, bf16[256,2,128]{2,0,1:T(8,128)(2,1)S(1)}, u32[]{:S(2)}, u32[]{:S(2)}) %collective-permute-start) | collective-permute-done | bytes 131104 | tf_op jit(solution)/shard_map/ppermute | solution.py:40
  95.0 10.3 %collective-permute-done.1 = bf16[256,2,128]{2,0,1:T(8,128)(2,1)S(1)} collective-permute-done((bf16[256,2,128]{2,0,1:T(8,128)(2,1)S(1)}, bf16[256,2,128]{2,0,1:T(8,128)(2,1)S(1)}, u32[]{:S(2)}, u32[]{:S(2)}) %collective-permute-start.1) | collective-permute-done | bytes 131104 | tf_op jit(solution)/shard_map/ppermute | solution.py:40
  105.4 10.5 %collective-permute-done.2 = bf16[256,2,128]{2,0,1:T(8,128)(2,1)S(1)} collective-permute-done((bf16[256,2,128]{2,0,1:T(8,128)(2,1)S(1)}, bf16[256,2,128]{2,0,1:T(8,128)(2,1)S(1)}, u32[]{:S(2)}, u32[]{:S(2)}) %collective-permute-start.2) | collective-permute-done | bytes 131104 | tf_op jit(solution)/shard_map/ppermute | solution.py:40
  116.1 7.5 %collective-permute-done.3 = bf16[256,2,128]{2,0,1:T(8,128)(2,1)S(1)} collective-permute-done((bf16[256,2,128]{2,0,1:T(8,128)(2,1)S(1)}, bf16[256,2,128]{2,0,1:T(8,128)(2,1)S(1)}, u32[]{:S(2)}, u32[]{:S(2)}) %collective-permute-start.3) | collective-permute-done | bytes 131104 | tf_op jit(solution)/shard_map/ppermute | solution.py:40
  123.6 36.2 %all-gather.5.cloned.1.call-done = bf16[7680,256]{1,0:T(8,128)(2,1)} async-done(((bf16[960,256]{1,0:T(8,128)(2,1)}), bf16[7680,256]{1,0:T(8,128)(2,1)}) %all-gather.5.cloned.1.call-update) | async-done | bytes 3932176 | tf_op jit(solution)/shard_map/all_gather | solution.py:50
  159.8 5.0 %multiply_reduce_fusion.1 = (f32[256,2]{0,1:T(2,128)S(1)}, f32[256,256]{0,1:T(8,128)S(1)}) fusion(bf16[256,7680]{1,0:T(8,128)(2,1)} %param.12, bf16[7680,256]{1,0:T(8,128)(2,1)} %all-gather.5.cloned.1.call-done), kind=kOutput, calls=%fused_computation.27 | convolution fusion | flops 1006763520 | bytes 8128512 | tf_op jit(solution)/shard_map/dot_general | solution.py:48
  164.9 1.1 collective-permute-start.5
  166.0 6.6 %collective-permute-done.5 = bf16[256,2,128]{2,0,1:T(8,128)(2,1)S(1)} collective-permute-done((bf16[256,2,128]{2,0,1:T(8,128)(2,1)S(1)}, bf16[256,2,128]{2,0,1:T(8,128)(2,1)S(1)}, u32[]{:S(2)}, u32[]{:S(2)}) %collective-permute-start.5) | collective-permute-done | bytes 131104 | tf_op jit(solution)/shard_map/ppermute | solution.py:40
  172.6 0.8 multiply_convert_fusion.1
  173.5 6.8 %collective-permute-done.6 = bf16[256,2,128]{2,0,1:T(8,128)(2,1)S(1)} collective-permute-done((bf16[256,2,128]{2,0,1:T(8,128)(2,1)S(1)}, bf16[256,2,128]{2,0,1:T(8,128)(2,1)S(1)}, u32[]{:S(2)}, u32[]{:S(2)}) %collective-permute-start.6) | collective-permute-done | bytes 131104 | tf_op jit(solution)/shard_map/ppermute | solution.py:40
  180.8 34.4 %all-gather.7.cloned.1.call-done = bf16[2048,2,128]{2,0,1:T(8,128)(2,1)} async-done(((bf16[256,2,128]{2,0,1:T(8,128)(2,1)}), bf16[2048,2,128]{2,0,1:T(8,128)(2,1)}) %all-gather.7.cloned.1.call-update) | async-done | bytes 1048592 | tf_op jit(solution)/shard_map/all_gather | solution.py:74
  215.2 8.5 %while.15 = (s32[]{:T(128)}, f32[32,2,8]{0,2,1:T(8,128)S(1)}, f32[32,2,8]{0,2,1:T(8,128)S(1)}, f32[32,2,8,128]{3,0,2,1:T(8,128)S(1)}, bf16[4,512,2,128]{3,1,0,2:...) while((s32[]{:T(128)}, f32[32,2,8]{0,2,1:T(8,128)S(1)}, ...), condition=%wide.region_5.6_spmd.clone, body=%wide.region_2.5_spmd.clone.sunk | while | flops 135989760 | bytes 4371053 | solution.py:103
  215.2 1.3 fusion.31
  216.5 0.3 fusion.32
  216.9 0.4 fusion.34
  217.3 1.3 fusion.31
  218.7 0.3 fusion.32
  219.0 0.4 fusion.34
  219.5 1.3 fusion.31
  221.2 0.4 fusion.34
  221.6 1.3 fusion.31
  223.3 0.4 fusion.34
  224.0 0.7 copy.44
  224.7 39.1 %all-gather.11.cloned.1.call-done = bf16[256,2048]{1,0:T(8,128)(2,1)} async-done(((bf16[32,2048]{1,0:T(8,128)(2,1)}), bf16[256,2048]{1,0:T(8,128)(2,1)}) %all-gather.11.cloned.1.call-update) | async-done | bytes 1048592 | tf_op jit(solution)/shard_map/all_gather | solution.py:112
  263.8 4.6 %convolution_convert_fusion = bf16[256,1024]{1,0:T(8,128)(2,1)} fusion(bf16[256,2048]{1,0:T(8,128)(2,1)} %all-gather.11.cloned.1.call-done, bf16[2048,1024]{1,0:T(8,128)(2,1)} %param.15), kind=kOutput, calls=%fused_computation.19 | convolution fusion | flops 1074003968 | bytes 5767168 | tf_op jit(solution)/shard_map/dot_general | solution.py:111
  269.1 6.1 %reduce-scatter.2.cloned.1.call-done = bf16[128,1024]{1,0:T(8,128)(2,1)} async-done(((bf16[256,1024]{1,0:T(8,128)(2,1)}), bf16[128,1024]{1,0:T(8,128)(2,1)}) %reduce-scatter.2.cloned.1.call-update) | async-done | bytes 262160 | tf_op jit(solution)/shard_map/reduce_scatter | solution.py:116
  275.2 1.7 add_convert_fusion
  (69 shorter events, 2.4 us)
Async XLA Ops:
  6.5 75.2 %all-gather.9.cloned.1.call-start = ((), (), s32[]{:S(2)}) async-start(), calls=%async_computation.3 | async-start | bytes 4423680 | tf_op jit(solution)/shard_map/all_gather | solution.py:55
  7.3 152.5 %all-gather.5.cloned.1.call-start = ((), (), s32[]{:S(2)}) async-start(), calls=%async_computation.1 | async-start | bytes 4423680 | tf_op jit(solution)/shard_map/all_gather | solution.py:50
  8.0 86.7 %copy-start.1 = (bf16[32,2048]{1,0:T(8,128)(2,1)S(1)}, bf16[32,2048]{1,0:T(8,128)(2,1)}, u32[]{:S(2)}) copy-start(bf16[32,2048]{1,0:T(8,128)(2,1)} %param.11) | copy-start | bytes 393220
  8.0 107.9 %copy-start.2 = (f32[128]{0:T(128)S(1)}, f32[128]{0:T(128)}, u32[]{:S(2)}) copy-start(f32[128]{0:T(128)} %param.17) | copy-start | bytes 1540
  8.0 207.2 %all-gather.7.cloned.1.call-start = ((), (), s32[]{:S(2)}) async-start(), calls=%async_computation.2 | async-start | bytes 1179648 | tf_op jit(solution)/shard_map/all_gather | solution.py:74
  86.8 7.8 %collective-permute-start = (bf16[256,2,128]{2,0,1:T(8,128)(2,1)S(1)}, bf16[256,2,128]{2,0,1:T(8,128)(2,1)S(1)}, u32[]{:S(2)}, u32[]{:S(2)}) collective-permute-start(bf16[256,2,128]{2,0,1:T(8,128)(2,1)S(1)} %copy.30), channel_id=1, source_target_pairs={{0,2},{2,4},{4,6},{6,8},{8,10},{10,12},{12,14},{14,0},{1,3},{3,5},... | collective-permute-start | bytes 393224 | tf_op jit(solution)/shard_map/ppermute | solution.py:40
  94.7 10.7 %collective-permute-start.1 = (bf16[256,2,128]{2,0,1:T(8,128)(2,1)S(1)}, bf16[256,2,128]{2,0,1:T(8,128)(2,1)S(1)}, u32[]{:S(2)}, u32[]{:S(2)}) collective-permute-start(bf16[256,2,128]{2,0,1:T(8,128)(2,1)S(1)} %collective-permute-done), channel_id=1, source_target_pairs={{0,2},{2,4},{4,6},{6,8},{8,10},{10,12},{12,14},{14,0},{1,3},{3,5},... | collective-permute-start | bytes 393224 | tf_op jit(solution)/shard_map/ppermute | solution.py:40
  105.3 10.6 %collective-permute-start.2 = (bf16[256,2,128]{2,0,1:T(8,128)(2,1)S(1)}, bf16[256,2,128]{2,0,1:T(8,128)(2,1)S(1)}, u32[]{:S(2)}, u32[]{:S(2)}) collective-permute-start(bf16[256,2,128]{2,0,1:T(8,128)(2,1)S(1)} %collective-permute-done.1), channel_id=1, source_target_pairs={{0,2},{2,4},{4,6},{6,8},{8,10},{10,12},{12,14},{14,0},{1,3},{3,5},... | collective-permute-start | bytes 393224 | tf_op jit(solution)/shard_map/ppermute | solution.py:40
  115.9 7.7 %collective-permute-start.3 = (bf16[256,2,128]{2,0,1:T(8,128)(2,1)S(1)}, bf16[256,2,128]{2,0,1:T(8,128)(2,1)S(1)}, u32[]{:S(2)}, u32[]{:S(2)}) collective-permute-start(bf16[256,2,128]{2,0,1:T(8,128)(2,1)S(1)} %collective-permute-done.2), channel_id=1, source_target_pairs={{0,2},{2,4},{4,6},{6,8},{8,10},{10,12},{12,14},{14,0},{1,3},{3,5},... | collective-permute-start | bytes 393224 | tf_op jit(solution)/shard_map/ppermute | solution.py:40
  116.1 56.5 %copy-start.3 = (f32[128]{0:T(128)S(1)}, f32[128]{0:T(128)}, u32[]{:S(2)}) copy-start(f32[128]{0:T(128)} %param.18) | copy-start | bytes 1540
  123.6 41.3 %collective-permute-start.4 = (bf16[256,2,128]{2,0,1:T(8,128)(2,1)S(1)}, bf16[256,2,128]{2,0,1:T(8,128)(2,1)S(1)}, u32[]{:S(2)}, u32[]{:S(2)}) collective-permute-start(bf16[256,2,128]{2,0,1:T(8,128)(2,1)S(1)} %collective-permute-done.3), channel_id=1, source_target_pairs={{0,2},{2,4},{4,6},{6,8},{8,10},{10,12},{12,14},{14,0},{1,3},{3,5},... | collective-permute-start | bytes 393224 | tf_op jit(solution)/shard_map/ppermute | solution.py:40
  164.9 7.7 %collective-permute-start.5 = (bf16[256,2,128]{2,0,1:T(8,128)(2,1)S(1)}, bf16[256,2,128]{2,0,1:T(8,128)(2,1)S(1)}, u32[]{:S(2)}, u32[]{:S(2)}) collective-permute-start(bf16[256,2,128]{2,0,1:T(8,128)(2,1)S(1)} %collective-permute-done.4), channel_id=1, source_target_pairs={{0,2},{2,4},{4,6},{6,8},{8,10},{10,12},{12,14},{14,0},{1,3},{3,5},... | collective-permute-start | bytes 393224 | tf_op jit(solution)/shard_map/ppermute | solution.py:40
  172.6 7.7 %collective-permute-start.6 = (bf16[256,2,128]{2,0,1:T(8,128)(2,1)S(1)}, bf16[256,2,128]{2,0,1:T(8,128)(2,1)S(1)}, u32[]{:S(2)}, u32[]{:S(2)}) collective-permute-start(bf16[256,2,128]{2,0,1:T(8,128)(2,1)S(1)} %collective-permute-done.5), channel_id=1, source_target_pairs={{0,2},{2,4},{4,6},{6,8},{8,10},{10,12},{12,14},{14,0},{1,3},{3,5},... | collective-permute-start | bytes 393224 | tf_op jit(solution)/shard_map/ppermute | solution.py:40
  173.4 90.4 %all-gather.11.cloned.1.call-start = ((), (), s32[]{:S(2)}) async-start(), calls=%async_computation.4 | async-start | bytes 1179648 | tf_op jit(solution)/shard_map/all_gather | solution.py:112
  224.7 50.5 %copy-start = (bf16[128,1024]{1,0:T(8,128)(2,1)S(1)}, bf16[128,1024]{1,0:T(8,128)(2,1)}, u32[]{:S(2)}) copy-start(bf16[128,1024]{1,0:T(8,128)(2,1)} %param.16) | copy-start | bytes 786436
  224.7 50.5 %reduce-scatter.2.cloned.1.call-start = ((), (), s32[]{:S(2)}) async-start(), calls=%async_computation.5 | async-start | bytes 786432 | tf_op jit(solution)/shard_map/reduce_scatter | solution.py:116
Sparse Core Ops, SparseCore 0:
  9.5 72.2 all-gather.8
  84.0 75.7 all-gather.4
  173.5 41.6 all-gather.6
  224.8 38.9 all-gather.10
  268.5 6.6 reduce-scatter.1
